TPU v7x, 256 devices: a whole 4x4x8 slice. The times are simulated.
256 devices in a mesh: row: 32 (over y, z), col: 8 (over x, core).
Axes of the slice: x: 4, y: 4, z: 8, core: 2. Of those that a mesh axis runs over, the one named last changes fastest.
Arguments:
- ancestor_inverse: float32 [12288, 12288], P('row', 'col'), may hold values from -5 to 320, as said below
- panel_one: float32 [12288, 256], P(('row', 'col')), may hold values from -0.015625 to 0.015625
- struct_one: int32 [10752], replicated, may hold values from 0 to 12287, as said below
- lower_one: float32 [256, 256], replicated, may hold values from -1 to 2, as said below
- panel_two: float32 [12288, 256], P(('row', 'col')), may hold values from -0.015625 to 0.015625
- struct_two: int32 [9216], replicated, may hold values from 0 to 12287, as said below
- panel_above: float32 [256, 256], replicated, may hold values from -0.375 to 0.375
- lower_two: float32 [256, 256], replicated, may hold values from -1 to 2, as said below
- tile_owner: int32 [1536, 1], P(('col', 'row')), may hold values from 0 to 7; in each aligned block of 6 rows (0 to 5, 6 to 11, ...) at most 2 rows name the same one
Outputs:
- inverse_one: float32 [12288, 256], P(('col', 'row'))
- diag_one: float32 [256, 256], replicated
- cross_two: float32 [256, 256], replicated
- diag_two: float32 [256, 256], replicated
- delivered: float32 [4096, 8, 256], P(('row', 'col'))
Inputs may be any that keep to these rules, and one draw needn't show every extreme that they name: ancestor_inverse is exactly symmetric and positive definite. `struct_one`: 10752 distinct row numbers of the ancestor block. `struct_two`: 9216 distinct entries of struct_one. `lower_one`: lower triangular with a positive diagonal. `lower_two`: lower triangular with a positive diagonal. `tile_owner`: within each aligned block of 6 entries (the tiles of one device) no value appears more than 2 times; in some block a value appears exactly 2 times.
All inputs are finite; a program needn't handle non-finite values.
Results may differ from a plain program's by a relative error of at most 0.00007.
Values sent between devices are 32-bit elements; how exact they have to be, the bound alone decides.
No kernel may reach another device: no remote copies, remote signals or barrier semaphores. Data moves between devices by JAX's collectives and lax.ppermute only.
A program may use at most 64 MiB of HBM per device.

v0:
```python
import jax
import jax.numpy as jnp
from jax import lax
from jax.sharding import Mesh
from jax.sharding import PartitionSpec as P

CAP = 2
COL = ("col_0", "col_1")
ROW = ("row_0", "row_1")
ROW_COL = ROW + COL
COL_ROW = COL + ROW
N_ROW = 32
N_COL = 8
N_Y, N_Z = (4, 8)


def row_mask(listed, start, count):
    rows = start + jnp.arange(count, dtype=jnp.int32)
    hit = listed[None, :] == rows[:, None]
    return jnp.max(jnp.where(hit, 1.0, 0.0), axis=1, keepdims=True)


def dot(left, right, dims=((1,), (0,)), precision=lax.Precision.HIGHEST):
    return lax.dot_general(
        left, right, (dims, ((), ())), precision=precision, preferred_element_type=jnp.float32
    )


def sum_at_owner(value, axis):
    count = lax.axis_size(axis)
    parts = value.reshape(count, value.shape[0] // count, *value.shape[1:])
    return jnp.sum(lax.all_to_all(parts, axis, 0, 0, tiled=True), axis=0)


def copies_of(value, axis):
    copies = jnp.broadcast_to(value[None], (lax.axis_size(axis), *value.shape))
    return lax.all_to_all(copies, axis, 0, 0, tiled=True)


def total(value):
    own = sum_at_owner(sum_at_owner(value, COL), ROW)
    over_row = copies_of(own, ROW).reshape(-1, value.shape[1])
    return copies_of(over_row, COL).reshape(value.shape)


def gather_moves():
    pairs = []
    for block in range(N_ROW * N_COL):
        column, place = divmod(block, N_ROW)
        z, y = divmod(place, N_Y)
        pairs.append((block, (y * N_Z + z) * N_COL + column))
    return pairs


def result_moves():
    pairs = []
    for block in range(N_ROW * N_COL):
        column, row = divmod(block, N_ROW)
        pairs.append((block, row * N_COL + column))
    return pairs


def deliver(values, tile_owner):
    tile_count = tile_owner.shape[0]
    tile_rows = values.shape[0] // tile_count
    all_tiles = values.reshape(tile_count, tile_rows, values.shape[1])
    owner = tile_owner[:, 0]
    order = jnp.arange(tile_count)
    same = (owner[:, None] == owner[None, :]) & (order[None, :] < order[:, None])
    rank = jnp.sum(same.astype(jnp.int32), axis=1)
    select = (
        (owner[None, None, :] == jnp.arange(N_COL)[:, None, None])
        & (rank[None, None, :] == jnp.arange(CAP)[None, :, None])
    ).astype(jnp.float32)
    outgoing = jnp.einsum("cks,srb->ckrb", select, all_tiles, precision=lax.Precision.HIGHEST)
    incoming = lax.all_to_all(outgoing, COL, split_axis=0, concat_axis=0, tiled=True)
    return incoming.reshape(N_COL * CAP, tile_rows, values.shape[1])


def local(
    ancestor_inverse,
    panel_one,
    struct_one,
    lower_one,
    panel_two,
    struct_two,
    panel_above,
    lower_two,
    tile_owner,
):
    row_index = lax.axis_index(ROW)
    col_index = lax.axis_index(COL)
    local_rows, width = panel_one.shape
    start = (row_index * N_COL + col_index) * local_rows
    mask_one = row_mask(struct_one, start, local_rows)
    mask_two = row_mask(struct_two, start, local_rows)
    panels = jnp.concatenate([panel_one * mask_one, panel_two * mask_two], axis=1)
    placed = lax.ppermute(panels, ROW_COL, gather_moves())
    column_panels = lax.all_gather(placed, "row_0", axis=0, tiled=True)
    column_panels = lax.all_gather(column_panels, "row_1", axis=0, tiled=True)
    row_panels = lax.all_gather(panels, COL, axis=0, tiled=True)
    product = dot(ancestor_inverse, column_panels, precision=lax.Precision.HIGH)
    from_one = dot(row_panels[:, :width], product, ((0,), (0,)), lax.Precision.HIGH)
    from_two = dot(row_panels[:, width:], product[:, width:], ((0,), (0,)), lax.Precision.HIGH)
    partial = jnp.concatenate([from_one[:, :width], from_one[:, width:], from_two], axis=0)
    grams = total(partial)
    w_one, w_cross, w_two = (grams[:width], grams[width : 2 * width], grams[2 * width :])
    diag_one = dot(lower_one, lower_one, ((0,), (0,))) + w_one
    cross_two = w_cross - dot(diag_one, panel_above)
    diag_two = (
        dot(lower_two, lower_two, ((0,), (0,)))
        + w_two
        - dot(w_cross, panel_above, ((0,), (0,)))
        - dot(panel_above, cross_two, ((0,), (0,)))
    )
    rows = sum_at_owner(product, COL)
    inverse_one = -rows[:, :width] * mask_one
    inverse_two = -(rows[:, width:] + dot(inverse_one, panel_above)) * mask_two
    inverses = lax.ppermute(
        jnp.concatenate([inverse_one, inverse_two], axis=1), ROW_COL, result_moves()
    )
    inverse_one, inverse_two = (inverses[:, :width], inverses[:, width:])
    delivered = deliver(inverse_two, tile_owner)
    return (inverse_one, diag_one, cross_two, diag_two, delivered)


def solution(mesh):
    finer = Mesh(mesh.devices.reshape(4, 8, 4, 2), ("row_0", "row_1", "col_0", "col_1"))
    return jax.shard_map(
        local,
        mesh=finer,
        in_specs=(
            P(ROW, COL),
            P(ROW_COL, None),
            P(),
            P(),
            P(ROW_COL, None),
            P(),
            P(),
            P(),
            P(COL_ROW, None),
        ),
        out_specs=(P(COL_ROW, None), P(), P(), P(), P(ROW_COL, None, None)),
        check_vma=False,
    )
```

profile of v0, /device:TPU:1, one launch (start us, length us, event | category | flops | bytes accessed | tf_op | source)
XLA Modules:
  0.0 209.6 jit_solution(13605550530463847932)
XLA Ops:
  7.2 1.3 select_reduce_fusion
  10.6 4.6 %collective-permute-start = (f32[48,512]{1,0:T(8,128)S(1)}, f32[48,512]{1,0:T(8,128)S(1)}, u32[]{:S(2)}, u32[]{:S(2)}) collective-permute-start(f32[48,512]{1,0:T(8,128)S(1)} %pad_maximum_fusion.1), channel_id=1, source_target_pairs={{0,0},{1,64},{2,128},{3,192},{4,8},{5,72},{6,136},{7,200},{8,16},{... | collective-permute-start | bytes 294920 | tf_op jit(solution)/shard_map/ppermute | solution.py:98
  15.2 8.1 %collective-permute-done = f32[48,512]{1,0:T(8,128)S(1)} collective-permute-done((f32[48,512]{1,0:T(8,128)S(1)}, f32[48,512]{1,0:T(8,128)S(1)}, u32[]{:S(2)}, u32[]{:S(2)}) %collective-permute-start) | collective-permute-done | bytes 98336 | tf_op jit(solution)/shard_map/ppermute | solution.py:98
  23.3 12.5 %all_gather.9 = f32[192,512]{1,0:T(8,128)} all-gather(f32[48,512]{1,0:T(8,128)S(1)} %collective-permute-done), channel_id=1, replica_groups=mesh['row_0'=4,'row_1'=8,'col_0'=4,'col_1'=2] {'row_0'}, dimensions={0}, use_global_device_ids=true | all-gather | bytes 491520 | tf_op jit(solution)/shard_map/all_gather | solution.py:99
  37.4 17.0 %all_gather.11 = f32[384,512]{1,0:T(8,128)} all-gather(f32[48,512]{1,0:T(8,128)S(1)} %pad_maximum_fusion.1), channel_id=1, replica_groups=mesh['row_0'=4,'row_1'=8,'col_0'=4,'col_1'=2] {'col_0','col_1'}, dimensions={0}, use_global_device_ids=true | all-gather | bytes 884736 | tf_op jit(solution)/shard_map/all_gather | solution.py:101
  54.4 34.5 %all-gather.2.cloned.1.call-done = f32[1536,512]{1,0:T(8,128)} async-done(((f32[192,512]{1,0:T(8,128)}), f32[1536,512]{1,0:T(8,128)}) %all-gather.2.cloned.1.call-update) | async-done | bytes 3145744 | tf_op jit(solution)/shard_map/all_gather | solution.py:100
  88.8 4.8 %fusion.19 = f32[512,384]{0,1:T(8,128)} fusion(f32[1536,512]{1,0:T(8,128)} %all-gather.2.cloned.1.call-done, f32[384,1536]{1,0:T(8,128)S(1)} %copy-done), kind=kOutput, calls=%fused_computation.39 | convolution fusion | flops 1811939328 | bytes 6291456 | tf_op jit(solution)/shard_map/dot_general | solution.py:24
  93.7 5.2 %all-to-all-start = ((f32[8,48,512]{2,1,0:T(8,128)}), f32[8,48,512]{2,1,0:T(8,128)S(1)}, u32[]{:S(2)}, u32[]{:S(2)}) async-start(f32[8,48,512]{2,1,0:T(8,128)} %bitcast.1), calls=%async_computation | async-start | bytes 1572864 | tf_op jit(solution)/shard_map/all_to_all | solution.py:32
  98.9 1.9 fusion.6
  100.9 1.5 fusion.3
  103.3 7.8 %all-to-all-done = f32[8,48,512]{2,1,0:T(8,128)S(1)} async-done(((f32[8,48,512]{2,1,0:T(8,128)}), f32[8,48,512]{2,1,0:T(8,128)S(1)}, u32[]{:S(2)}, u32[]{:S(2)}) %all-to-all-start) | async-done | bytes 786464 | tf_op jit(solution)/shard_map/all_to_all | solution.py:32
  111.1 5.0 %all-to-all-start.1 = ((f32[8,96,256]{2,1,0:T(8,128)}), f32[8,96,256]{2,1,0:T(8,128)}, u32[]{:S(2)}, u32[]{:S(2)}) async-start(f32[8,96,256]{2,1,0:T(8,128)} %bitcast.2), calls=%async_computation.1 | async-start | bytes 1572864 | tf_op jit(solution)/shard_map/all_to_all | solution.py:32
  116.5 2.9 %collective-permute-start.1 = (f32[48,512]{1,0:T(8,128)S(1)}, f32[48,512]{1,0:T(8,128)S(1)}, u32[]{:S(2)}, u32[]{:S(2)}) collective-permute-start(f32[48,512]{1,0:T(8,128)S(1)} %pad_maximum_fusion.2), channel_id=1, source_target_pairs={{0,0},{1,8},{2,16},{3,24},{4,32},{5,40},{6,48},{7,56},{8,64},{9,72... | collective-permute-start | bytes 294920 | tf_op jit(solution)/shard_map/ppermute | solution.py:119
  119.4 9.1 %all-to-all-done.1 = f32[8,96,256]{2,1,0:T(8,128)} async-done(((f32[8,96,256]{2,1,0:T(8,128)}), f32[8,96,256]{2,1,0:T(8,128)}, u32[]{:S(2)}, u32[]{:S(2)}) %all-to-all-start.1) | async-done | bytes 786464 | tf_op jit(solution)/shard_map/all_to_all | solution.py:32
  130.4 14.0 %all-to-all-start.2 = ((f32[32,3,256]{2,1,0:T(4,128)}), f32[32,3,256]{2,1,0:T(4,128)S(1)}, u32[]{:S(2)}, u32[]{:S(2)}) async-start(f32[32,3,256]{2,1,0:T(4,128)} %reshape.90), calls=%async_computation.2 | async-start | bytes 262144 | tf_op jit(solution)/shard_map/all_to_all | solution.py:32
  145.1 8.5 %all-to-all-done.2 = f32[32,3,256]{2,1,0:T(4,128)S(1)} async-done(((f32[32,3,256]{2,1,0:T(4,128)}), f32[32,3,256]{2,1,0:T(4,128)S(1)}, u32[]{:S(2)}, u32[]{:S(2)}) %all-to-all-start.2) | async-done | bytes 98336 | tf_op jit(solution)/shard_map/all_to_all | solution.py:32
  154.3 3.9 %all-to-all-start.3 = ((f32[32,3,256]{2,1,0:T(4,128)}), f32[32,3,256]{2,1,0:T(4,128)S(1)}, u32[]{:S(2)}, u32[]{:S(2)}) async-start(f32[32,3,256]{2,1,0:T(4,128)} %broadcast_in_dim.44), calls=%async_computation.3 | async-start | bytes 262144 | tf_op jit(solution)/shard_map/all_to_all | solution.py:37
  159.1 8.3 %all-to-all-done.3 = f32[32,3,256]{2,1,0:T(4,128)S(1)} async-done(((f32[32,3,256]{2,1,0:T(4,128)}), f32[32,3,256]{2,1,0:T(4,128)S(1)}, u32[]{:S(2)}, u32[]{:S(2)}) %all-to-all-start.3) | async-done | bytes 98336 | tf_op jit(solution)/shard_map/all_to_all | solution.py:37
  167.3 7.3 %all-to-all-start.5 = ((f32[8,2,8,256]{3,2,1,0:T(8,128)}), f32[8,2,8,256]{3,2,1,0:T(8,128)S(1)}, u32[]{:S(2)}, u32[]{:S(2)}) async-start(f32[8,2,8,256]{3,2,1,0:T(8,128)} %copy.24), calls=%async_computation.5 | async-start | bytes 262144 | tf_op jit(solution)/shard_map/all_to_all | solution.py:76
  174.7 5.2 %all-to-all-done.5 = f32[8,2,8,256]{3,2,1,0:T(8,128)S(1)} async-done(((f32[8,2,8,256]{3,2,1,0:T(8,128)}), f32[8,2,8,256]{3,2,1,0:T(8,128)S(1)}, u32[]{:S(2)}, u32[]{:S(2)}) %all-to-all-start.5) | async-done | bytes 131104 | tf_op jit(solution)/shard_map/all_to_all | solution.py:76
  180.9 4.3 %all-to-all-start.4 = ((f32[8,96,256]{2,1,0:T(8,128)}), f32[8,96,256]{2,1,0:T(8,128)S(1)}, u32[]{:S(2)}, u32[]{:S(2)}) async-start(f32[8,96,256]{2,1,0:T(8,128)} %broadcast_in_dim.46), calls=%async_computation.4 | async-start | bytes 1572864 | tf_op jit(solution)/shard_map/all_to_all | solution.py:37
  185.2 12.3 %all-to-all-done.4 = f32[8,96,256]{2,1,0:T(8,128)S(1)} async-done(((f32[8,96,256]{2,1,0:T(8,128)}), f32[8,96,256]{2,1,0:T(8,128)S(1)}, u32[]{:S(2)}, u32[]{:S(2)}) %all-to-all-start.4) | async-done | bytes 786464 | tf_op jit(solution)/shard_map/all_to_all | solution.py:37
  197.5 1.7 convolution_add_fusion
  200.8 1.3 fusion
  (41 shorter events, 12.4 us)
Async XLA Ops:
  7.2 81.7 %copy-start = (f32[384,1536]{1,0:T(8,128)S(1)}, f32[384,1536]{1,0:T(8,128)}, u32[]{:S(2)}) copy-start(f32[384,1536]{1,0:T(8,128)} %param.9) | copy-start | bytes 7077892
  7.2 81.7 %all-gather.2.cloned.1.call-start = ((), (), s32[]{:S(2)}) async-start(), calls=%async_computation.6 | async-start | bytes 3538944 | tf_op jit(solution)/shard_map/all_gather | solution.py:100
  10.6 12.7 %collective-permute-start = (f32[48,512]{1,0:T(8,128)S(1)}, f32[48,512]{1,0:T(8,128)S(1)}, u32[]{:S(2)}, u32[]{:S(2)}) collective-permute-start(f32[48,512]{1,0:T(8,128)S(1)} %pad_maximum_fusion.1), channel_id=1, source_target_pairs={{0,0},{1,64},{2,128},{3,192},{4,8},{5,72},{6,136},{7,200},{8,16},{... | collective-permute-start | bytes 294920 | tf_op jit(solution)/shard_map/ppermute | solution.py:98
  93.7 17.4 %all-to-all-start = ((f32[8,48,512]{2,1,0:T(8,128)}), f32[8,48,512]{2,1,0:T(8,128)S(1)}, u32[]{:S(2)}, u32[]{:S(2)}) async-start(f32[8,48,512]{2,1,0:T(8,128)} %bitcast.1), calls=%async_computation | async-start | bytes 1572864 | tf_op jit(solution)/shard_map/all_to_all | solution.py:32
  98.9 2.0 copy-start.2
  102.4 13.9 %copy-start.1 = (f32[256,256]{1,0:T(8,128)S(1)}, f32[256,256]{1,0:T(8,128)}, u32[]{:S(2)}) copy-start(f32[256,256]{1,0:T(8,128)} %param.15) | copy-start | bytes 786436
  111.1 17.4 %all-to-all-start.1 = ((f32[8,96,256]{2,1,0:T(8,128)}), f32[8,96,256]{2,1,0:T(8,128)}, u32[]{:S(2)}, u32[]{:S(2)}) async-start(f32[8,96,256]{2,1,0:T(8,128)} %bitcast.2), calls=%async_computation.1 | async-start | bytes 1572864 | tf_op jit(solution)/shard_map/all_to_all | solution.py:32
  116.5 27.9 %collective-permute-start.1 = (f32[48,512]{1,0:T(8,128)S(1)}, f32[48,512]{1,0:T(8,128)S(1)}, u32[]{:S(2)}, u32[]{:S(2)}) collective-permute-start(f32[48,512]{1,0:T(8,128)S(1)} %pad_maximum_fusion.2), channel_id=1, source_target_pairs={{0,0},{1,8},{2,16},{3,24},{4,32},{5,40},{6,48},{7,56},{8,64},{9,72... | collective-permute-start | bytes 294920 | tf_op jit(solution)/shard_map/ppermute | solution.py:119
  130.4 23.2 %all-to-all-start.2 = ((f32[32,3,256]{2,1,0:T(4,128)}), f32[32,3,256]{2,1,0:T(4,128)S(1)}, u32[]{:S(2)}, u32[]{:S(2)}) async-start(f32[32,3,256]{2,1,0:T(4,128)} %reshape.90), calls=%async_computation.2 | async-start | bytes 262144 | tf_op jit(solution)/shard_map/all_to_all | solution.py:32
  154.3 13.0 %all-to-all-start.3 = ((f32[32,3,256]{2,1,0:T(4,128)}), f32[32,3,256]{2,1,0:T(4,128)S(1)}, u32[]{:S(2)}, u32[]{:S(2)}) async-start(f32[32,3,256]{2,1,0:T(4,128)} %broadcast_in_dim.44), calls=%async_computation.3 | async-start | bytes 262144 | tf_op jit(solution)/shard_map/all_to_all | solution.py:37
  167.3 12.6 %all-to-all-start.5 = ((f32[8,2,8,256]{3,2,1,0:T(8,128)}), f32[8,2,8,256]{3,2,1,0:T(8,128)S(1)}, u32[]{:S(2)}, u32[]{:S(2)}) async-start(f32[8,2,8,256]{3,2,1,0:T(8,128)} %copy.24), calls=%async_computation.5 | async-start | bytes 262144 | tf_op jit(solution)/shard_map/all_to_all | solution.py:76
  180.9 16.6 %all-to-all-start.4 = ((f32[8,96,256]{2,1,0:T(8,128)}), f32[8,96,256]{2,1,0:T(8,128)S(1)}, u32[]{:S(2)}, u32[]{:S(2)}) async-start(f32[8,96,256]{2,1,0:T(8,128)} %broadcast_in_dim.46), calls=%async_computation.4 | async-start | bytes 1572864 | tf_op jit(solution)/shard_map/all_to_all | solution.py:37
  197.5 2.3 %copy-start.3 = (f32[256,256]{1,0:T(8,128)S(1)}, f32[256,256]{1,0:T(8,128)}, u32[]{:S(2)}) copy-start(f32[256,256]{1,0:T(8,128)} %param.12) | copy-start | bytes 786436
  200.4 2.4 %copy-start.4 = (f32[256,256]{1,0:T(8,128)}, f32[256,256]{1,0:T(8,128)S(1)}, u32[]{:S(2)}) copy-start(f32[256,256]{1,0:T(8,128)S(1)} %convolution_add_fusion.1) | copy-start | bytes 786436
  200.8 2.0 copy-start.5
Sparse Core Ops, SparseCore 0:
  35.9 52.8 all-gather.1
where the time goes:
time: 211 us; the launch traced here: 210 us
  waiting for transfers between devices  93.9 us (45%)
  starting transfers between devices  47.1 us (22%)
  blocking collectives  29.4 us (14%)
  between operations  14.3 us (7%)
  matrix products  13.3 us (6%)
  other arithmetic  7.24 us (3%)
  local copies, waits for them, and re-layouts  4.43 us (2%)
    all_gather x1, waiting for transfers between devices, local(): column_panels = lax.all_gather(column_panels, 'row_1', axis=0, tiled=True)  34.5 us
    all_to_all x3, waiting for transfers between devices, sum_at_owner(): return jnp.sum(lax.all_to_all(parts, axis, 0, 0, tiled=True), axis=0)  25.5 us
    all_to_all x3, starting transfers between devices, sum_at_owner(): return jnp.sum(lax.all_to_all(parts, axis, 0, 0, tiled=True), axis=0)  24.1 us
    all_to_all x2, waiting for transfers between devices, copies_of(): return lax.all_to_all(copies, axis, 0, 0, tiled=True)  20.6 us
    all_gather x1, blocking collectives, local(): row_panels = lax.all_gather(panels, COL, axis=0, tiled=True)  17 us
    dot_general x9, matrix products, dot(): lax.dot_general(left, right, (dims, ((), ())), precision=precision, prefe...  13.1 us
    all_gather x1, blocking collectives, local(): column_panels = lax.all_gather(placed, 'row_0', axis=0, tiled=True)  12.5 us
    all_to_all x2, starting transfers between devices, copies_of(): return lax.all_to_all(copies, axis, 0, 0, tiled=True)  8.17 us
  transfers between devices with their start and end apart: 9, of which 8 were waited for; matrix products, arithmetic and copies ran while one was open for 5% of the time, Pallas kernels for 0%

commit v1 on v0

--- a/solution.py
+++ b/solution.py
@@ -3,6 +3,7 @@
 from jax import lax
 from jax.sharding import Mesh
 from jax.sharding import PartitionSpec as P
+from jax.lax import all_to_all, psum
 
 CAP = 2
 COL = ("col_0", "col_1")
@@ -97,7 +98,9 @@
     panels = jnp.concatenate([panel_one * mask_one, panel_two * mask_two], axis=1)
     placed = lax.ppermute(panels, ROW_COL, gather_moves())
     column_panels = lax.all_gather(placed, "row_0", axis=0, tiled=True)
-    column_panels = lax.all_gather(column_panels, "row_1", axis=0, tiled=True)
+    column_panels = jnp.concatenate(
+        all_to_all(jnp.stack([column_panels] * psum(1, "row_1")), "row_1", 0, 0), axis=0
+    )
     row_panels = lax.all_gather(panels, COL, axis=0, tiled=True)
     product = dot(ancestor_inverse, column_panels, precision=lax.Precision.HIGH)
     from_one = dot(row_panels[:, :width], product, ((0,), (0,)), lax.Precision.HIGH)

time: 211 us -> 226 us (1.071)
  between operations: 14.3 us -> 0.87 us
  waiting for transfers between devices: 93.9 us -> 107 us
  starting transfers between devices: 47.1 us -> 57.2 us
  blocking collectives: 29.4 us -> 33.5 us
    all_to_all x0 -> x1, waiting for transfers between devices: none -> 47.5 us  [local(): all_to_all(jnp.stack([column_panels] * psum(1, 'row_1')), 'row_1', 0, 0)]
    all_gather x1 -> x0, waiting for transfers between devices: 34.5 us -> none  [local(): column_panels = lax.all_gather(column_panels, 'row_1', axis=0, tiled=True)]
    all_to_all x0 -> x1, starting transfers between devices: none -> 9.06 us  [local(): all_to_all(jnp.stack([column_panels] * psum(1, 'row_1')), 'row_1', 0, 0)]
    all_gather x1, blocking collectives: 17 us -> 21.7 us  [local(): row_panels = lax.all_gather(panels, COL, axis=0, tiled=True)]
  transfers between devices with their start and end apart: 9 -> 9, of which waited for: 8 -> 8; matrix products, arithmetic and copies ran while one was open for 5% -> 4% of each run, Pallas kernels for 0% -> 0%
where the time goes in v1:
time: 226 us; the launch traced here: 225 us
  waiting for transfers between devices  107 us (47%)
  starting transfers between devices  57.2 us (25%)
  blocking collectives  33.5 us (15%)
  matrix products  13.3 us (6%)
  local copies, waits for them, and re-layouts  6.53 us (3%)
  other arithmetic  5.86 us (3%)
    all_to_all x1, waiting for transfers between devices, local(): all_to_all(jnp.stack([column_panels] * psum(1, 'row_1')), 'row_1', 0, 0)  47.5 us
    all_to_all x3, waiting for transfers between devices, sum_at_owner(): return jnp.sum(lax.all_to_all(parts, axis, 0, 0, tiled=True), axis=0)  26.1 us
    all_to_all x3, starting transfers between devices, sum_at_owner(): return jnp.sum(lax.all_to_all(parts, axis, 0, 0, tiled=True), axis=0)  25.8 us
    all_gather x1, blocking collectives, local(): row_panels = lax.all_gather(panels, COL, axis=0, tiled=True)  21.7 us
    all_to_all x2, waiting for transfers between devices, copies_of(): return lax.all_to_all(copies, axis, 0, 0, tiled=True)  20.6 us
    dot_general x9, matrix products, dot(): lax.dot_general(left, right, (dims, ((), ())), precision=precision, prefe...  13.1 us
    all_gather x1, blocking collectives, local(): column_panels = lax.all_gather(placed, 'row_0', axis=0, tiled=True)  11.7 us
    all_to_all x1, starting transfers between devices, local(): all_to_all(jnp.stack([column_panels] * psum(1, 'row_1')), 'row_1', 0, 0)  9.06 us
  transfers between devices with their start and end apart: 9, of which 8 were waited for; matrix products, arithmetic and copies ran while one was open for 4% of the time, Pallas kernels for 0%

profile of v1, /device:TPU:1, one launch (start us, length us, event | category | flops | bytes accessed | tf_op | source)
XLA Modules:
  0.0 224.7 jit_solution(9630679193038962177)
XLA Ops:
  4.0 4.6 %collective-permute-start = (f32[48,512]{1,0:T(8,128)S(1)}, f32[48,512]{1,0:T(8,128)S(1)}, u32[]{:S(2)}, u32[]{:S(2)}) collective-permute-start(f32[48,512]{1,0:T(8,128)S(1)} %pad_maximum_fusion.1), channel_id=1, source_target_pairs={{0,0},{1,64},{2,128},{3,192},{4,8},{5,72},{6,136},{7,200},{8,16},{... | collective-permute-start | bytes 294920 | tf_op jit(solution)/shard_map/ppermute | solution.py:99
  8.6 8.1 %collective-permute-done = f32[48,512]{1,0:T(8,128)S(1)} collective-permute-done((f32[48,512]{1,0:T(8,128)S(1)}, f32[48,512]{1,0:T(8,128)S(1)}, u32[]{:S(2)}, u32[]{:S(2)}) %collective-permute-start) | collective-permute-done | bytes 98336 | tf_op jit(solution)/shard_map/ppermute | solution.py:99
  16.7 11.7 %all_gather.6 = f32[192,512]{1,0:T(8,128)S(1)} all-gather(f32[48,512]{1,0:T(8,128)S(1)} %collective-permute-done), channel_id=1, replica_groups=mesh['row_0'=4,'row_1'=8,'col_0'=4,'col_1'=2] {'row_0'}, dimensions={0}, use_global_device_ids=true | all-gather | bytes 491520 | tf_op jit(solution)/shard_map/all_gather | solution.py:100
  28.4 2.1 stack.2
  30.5 9.1 %all-to-all-start = ((f32[8,192,512]{2,1,0:T(8,128)}), f32[8,192,512]{2,1,0:T(8,128)}, u32[]{:S(2)}, u32[]{:S(2)}) async-start(f32[8,192,512]{2,1,0:T(8,128)} %stack.2), calls=%async_computation | async-start | bytes 6291456 | tf_op jit(solution)/shard_map/all_to_all | solution.py:102
  39.8 21.7 %all_gather.7 = f32[384,512]{1,0:T(8,128)} all-gather(f32[48,512]{1,0:T(8,128)S(1)} %pad_maximum_fusion.1), channel_id=1, replica_groups=mesh['row_0'=4,'row_1'=8,'col_0'=4,'col_1'=2] {'col_0','col_1'}, dimensions={0}, use_global_device_ids=true | all-gather | bytes 884736 | tf_op jit(solution)/shard_map/all_gather | solution.py:104
  61.5 47.5 %all-to-all-done = f32[8,192,512]{2,1,0:T(8,128)} async-done(((f32[8,192,512]{2,1,0:T(8,128)}), f32[8,192,512]{2,1,0:T(8,128)}, u32[]{:S(2)}, u32[]{:S(2)}) %all-to-all-start) | async-done | bytes 3145760 | tf_op jit(solution)/shard_map/all_to_all | solution.py:102
  109.0 4.8 %fusion.19 = f32[512,384]{0,1:T(8,128)} fusion(f32[1536,512]{1,0:T(8,128)} %bitcast, f32[384,1536]{1,0:T(8,128)S(1)} %copy-done), kind=kOutput, calls=%fused_computation.39 | convolution fusion | flops 1811939328 | bytes 6291456 | tf_op jit(solution)/shard_map/dot_general | solution.py:25
  113.8 11.5 %all-to-all-start.1 = ((f32[8,48,512]{2,1,0:T(8,128)}), f32[8,48,512]{2,1,0:T(8,128)S(1)}, u32[]{:S(2)}, u32[]{:S(2)}) async-start(f32[8,48,512]{2,1,0:T(8,128)} %bitcast.2), calls=%async_computation.1 | async-start | bytes 1572864 | tf_op jit(solution)/shard_map/all_to_all | solution.py:33
  125.4 1.9 fusion.6
  127.4 1.5 fusion.3
  129.8 7.8 %all-to-all-done.1 = f32[8,48,512]{2,1,0:T(8,128)S(1)} async-done(((f32[8,48,512]{2,1,0:T(8,128)}), f32[8,48,512]{2,1,0:T(8,128)S(1)}, u32[]{:S(2)}, u32[]{:S(2)}) %all-to-all-start.1) | async-done | bytes 786464 | tf_op jit(solution)/shard_map/all_to_all | solution.py:33
  137.6 5.0 %all-to-all-start.2 = ((f32[8,96,256]{2,1,0:T(8,128)}), f32[8,96,256]{2,1,0:T(8,128)}, u32[]{:S(2)}, u32[]{:S(2)}) async-start(f32[8,96,256]{2,1,0:T(8,128)} %bitcast.3), calls=%async_computation.2 | async-start | bytes 1572864 | tf_op jit(solution)/shard_map/all_to_all | solution.py:33
  143.0 2.2 collective-permute-start.1
  145.2 9.8 %all-to-all-done.2 = f32[8,96,256]{2,1,0:T(8,128)} async-done(((f32[8,96,256]{2,1,0:T(8,128)}), f32[8,96,256]{2,1,0:T(8,128)}, u32[]{:S(2)}, u32[]{:S(2)}) %all-to-all-start.2) | async-done | bytes 786464 | tf_op jit(solution)/shard_map/all_to_all | solution.py:33
  156.9 9.3 %all-to-all-start.3 = ((f32[32,3,256]{2,1,0:T(4,128)}), f32[32,3,256]{2,1,0:T(4,128)S(1)}, u32[]{:S(2)}, u32[]{:S(2)}) async-start(f32[32,3,256]{2,1,0:T(4,128)} %reshape.96), calls=%async_computation.3 | async-start | bytes 262144 | tf_op jit(solution)/shard_map/all_to_all | solution.py:33
  166.9 8.5 %all-to-all-done.3 = f32[32,3,256]{2,1,0:T(4,128)S(1)} async-done(((f32[32,3,256]{2,1,0:T(4,128)}), f32[32,3,256]{2,1,0:T(4,128)S(1)}, u32[]{:S(2)}, u32[]{:S(2)}) %all-to-all-start.3) | async-done | bytes 98336 | tf_op jit(solution)/shard_map/all_to_all | solution.py:33
  176.1 3.9 %all-to-all-start.4 = ((f32[32,3,256]{2,1,0:T(4,128)}), f32[32,3,256]{2,1,0:T(4,128)S(1)}, u32[]{:S(2)}, u32[]{:S(2)}) async-start(f32[32,3,256]{2,1,0:T(4,128)} %broadcast_in_dim.44), calls=%async_computation.4 | async-start | bytes 262144 | tf_op jit(solution)/shard_map/all_to_all | solution.py:38
  180.9 8.2 %all-to-all-done.4 = f32[32,3,256]{2,1,0:T(4,128)S(1)} async-done(((f32[32,3,256]{2,1,0:T(4,128)}), f32[32,3,256]{2,1,0:T(4,128)S(1)}, u32[]{:S(2)}, u32[]{:S(2)}) %all-to-all-start.4) | async-done | bytes 98336 | tf_op jit(solution)/shard_map/all_to_all | solution.py:38
  189.1 7.4 %all-to-all-start.6 = ((f32[8,2,8,256]{3,2,1,0:T(8,128)}), f32[8,2,8,256]{3,2,1,0:T(8,128)S(1)}, u32[]{:S(2)}, u32[]{:S(2)}) async-start(f32[8,2,8,256]{3,2,1,0:T(8,128)} %copy.24), calls=%async_computation.6 | async-start | bytes 262144 | tf_op jit(solution)/shard_map/all_to_all | solution.py:77
  196.6 5.2 %all-to-all-done.6 = f32[8,2,8,256]{3,2,1,0:T(8,128)S(1)} async-done(((f32[8,2,8,256]{3,2,1,0:T(8,128)}), f32[8,2,8,256]{3,2,1,0:T(8,128)S(1)}, u32[]{:S(2)}, u32[]{:S(2)}) %all-to-all-start.6) | async-done | bytes 131104 | tf_op jit(solution)/shard_map/all_to_all | solution.py:77
  202.8 4.3 %all-to-all-start.5 = ((f32[8,96,256]{2,1,0:T(8,128)}), f32[8,96,256]{2,1,0:T(8,128)S(1)}, u32[]{:S(2)}, u32[]{:S(2)}) async-start(f32[8,96,256]{2,1,0:T(8,128)} %broadcast_in_dim.46), calls=%async_computation.5 | async-start | bytes 1572864 | tf_op jit(solution)/shard_map/all_to_all | solution.py:38
  207.1 12.3 %all-to-all-done.5 = f32[8,96,256]{2,1,0:T(8,128)S(1)} async-done(((f32[8,96,256]{2,1,0:T(8,128)}), f32[8,96,256]{2,1,0:T(8,128)S(1)}, u32[]{:S(2)}, u32[]{:S(2)}) %all-to-all-start.5) | async-done | bytes 786464 | tf_op jit(solution)/shard_map/all_to_all | solution.py:38
  219.4 1.7 convolution_add_fusion
  (43 shorter events, 13.6 us)
Async XLA Ops:
  0.6 108.4 %copy-start = (f32[384,1536]{1,0:T(8,128)S(1)}, f32[384,1536]{1,0:T(8,128)}, u32[]{:S(2)}) copy-start(f32[384,1536]{1,0:T(8,128)} %param.9) | copy-start | bytes 7077892
  4.0 12.7 %collective-permute-start = (f32[48,512]{1,0:T(8,128)S(1)}, f32[48,512]{1,0:T(8,128)S(1)}, u32[]{:S(2)}, u32[]{:S(2)}) collective-permute-start(f32[48,512]{1,0:T(8,128)S(1)} %pad_maximum_fusion.1), channel_id=1, source_target_pairs={{0,0},{1,64},{2,128},{3,192},{4,8},{5,72},{6,136},{7,200},{8,16},{... | collective-permute-start | bytes 294920 | tf_op jit(solution)/shard_map/ppermute | solution.py:99
  30.5 9.1 %copy-start.6 = (s32[6,1]{0,1:T(1,128)S(1)}, s32[6,1]{0,1:T(1,128)}, u32[]{:S(2)}) copy-start(s32[6,1]{0,1:T(1,128)} %param.17) | copy-start | bytes 76
  30.5 78.5 %all-to-all-start = ((f32[8,192,512]{2,1,0:T(8,128)}), f32[8,192,512]{2,1,0:T(8,128)}, u32[]{:S(2)}, u32[]{:S(2)}) async-start(f32[8,192,512]{2,1,0:T(8,128)} %stack.2), calls=%async_computation | async-start | bytes 6291456 | tf_op jit(solution)/shard_map/all_to_all | solution.py:102
  113.8 23.8 %all-to-all-start.1 = ((f32[8,48,512]{2,1,0:T(8,128)}), f32[8,48,512]{2,1,0:T(8,128)S(1)}, u32[]{:S(2)}, u32[]{:S(2)}) async-start(f32[8,48,512]{2,1,0:T(8,128)} %bitcast.2), calls=%async_computation.1 | async-start | bytes 1572864 | tf_op jit(solution)/shard_map/all_to_all | solution.py:33
  125.4 2.0 copy-start.2
  128.9 13.9 %copy-start.1 = (f32[256,256]{1,0:T(8,128)S(1)}, f32[256,256]{1,0:T(8,128)}, u32[]{:S(2)}) copy-start(f32[256,256]{1,0:T(8,128)} %param.15) | copy-start | bytes 786436
  137.6 17.4 %all-to-all-start.2 = ((f32[8,96,256]{2,1,0:T(8,128)}), f32[8,96,256]{2,1,0:T(8,128)}, u32[]{:S(2)}, u32[]{:S(2)}) async-start(f32[8,96,256]{2,1,0:T(8,128)} %bitcast.3), calls=%async_computation.2 | async-start | bytes 1572864 | tf_op jit(solution)/shard_map/all_to_all | solution.py:33
  143.0 23.2 %collective-permute-start.1 = (f32[48,512]{1,0:T(8,128)S(1)}, f32[48,512]{1,0:T(8,128)S(1)}, u32[]{:S(2)}, u32[]{:S(2)}) collective-permute-start(f32[48,512]{1,0:T(8,128)S(1)} %pad_maximum_fusion.2), channel_id=1, source_target_pairs={{0,0},{1,8},{2,16},{3,24},{4,32},{5,40},{6,48},{7,56},{8,64},{9,72... | collective-permute-start | bytes 294920 | tf_op jit(solution)/shard_map/ppermute | solution.py:122
  156.9 18.5 %all-to-all-start.3 = ((f32[32,3,256]{2,1,0:T(4,128)}), f32[32,3,256]{2,1,0:T(4,128)S(1)}, u32[]{:S(2)}, u32[]{:S(2)}) async-start(f32[32,3,256]{2,1,0:T(4,128)} %reshape.96), calls=%async_computation.3 | async-start | bytes 262144 | tf_op jit(solution)/shard_map/all_to_all | solution.py:33
  176.1 13.0 %all-to-all-start.4 = ((f32[32,3,256]{2,1,0:T(4,128)}), f32[32,3,256]{2,1,0:T(4,128)S(1)}, u32[]{:S(2)}, u32[]{:S(2)}) async-start(f32[32,3,256]{2,1,0:T(4,128)} %broadcast_in_dim.44), calls=%async_computation.4 | async-start | bytes 262144 | tf_op jit(solution)/shard_map/all_to_all | solution.py:38
  189.1 12.7 %all-to-all-start.6 = ((f32[8,2,8,256]{3,2,1,0:T(8,128)}), f32[8,2,8,256]{3,2,1,0:T(8,128)S(1)}, u32[]{:S(2)}, u32[]{:S(2)}) async-start(f32[8,2,8,256]{3,2,1,0:T(8,128)} %copy.24), calls=%async_computation.6 | async-start | bytes 262144 | tf_op jit(solution)/shard_map/all_to_all | solution.py:77
  202.8 16.6 %all-to-all-start.5 = ((f32[8,96,256]{2,1,0:T(8,128)}), f32[8,96,256]{2,1,0:T(8,128)S(1)}, u32[]{:S(2)}, u32[]{:S(2)}) async-start(f32[8,96,256]{2,1,0:T(8,128)} %broadcast_in_dim.46), calls=%async_computation.5 | async-start | bytes 1572864 | tf_op jit(solution)/shard_map/all_to_all | solution.py:38
  219.4 2.3 %copy-start.3 = (f32[256,256]{1,0:T(8,128)S(1)}, f32[256,256]{1,0:T(8,128)}, u32[]{:S(2)}) copy-start(f32[256,256]{1,0:T(8,128)} %param.12) | copy-start | bytes 786436
  222.3 2.4 %copy-start.4 = (f32[256,256]{1,0:T(8,128)}, f32[256,256]{1,0:T(8,128)S(1)}, u32[]{:S(2)}) copy-start(f32[256,256]{1,0:T(8,128)S(1)} %convolution_add_fusion.1) | copy-start | bytes 786436
  222.7 2.0 copy-start.5
